TPU v7x, 128 devices: a whole 4x4x4 slice. The times are simulated.
128 devices in a mesh: gr: 16 (over x, y), gc: 8 (over z, core).
Axes of the slice: x: 4, y: 4, z: 4, core: 2. Of those that a mesh axis runs over, the one named last changes fastest.
Arguments:
- child_rows: float32 [8192, 12288], P('gr', 'gc'), may hold values from -1.5 to 1.5
- row_map: int32 [8192], P('gr'), may hold values from 0 to 8191, as said below
- stair: int32 [64], replicated, may hold values from 0 to 896, as said below
Outputs:
- factor: float32 [1024, 12288], P('gr', 'gc')
- projected: float32 [8192, 12288], P('gr', 'gc')
Inputs may be any that keep to these rules, and one draw needn't show every extreme that they name: row_map is a permutation of 0 to 8191. Of the 512 rows of one index of gr, at most 152 go to the rows of any one index of gr (row_map // 512), and some index of gr sends exactly 152 to one index. stair is nondecreasing and a multiple of 128; the first quarter of the blocks is 0 and the last block holds 896.
All inputs are finite; a program needn't handle non-finite values.
Results may differ from a plain program's by a relative error of at most 0.0003.
Values sent between devices are 32-bit elements; how exact they have to be, the bound alone decides.
A program may use at most 128 MiB of HBM per device.

v0:
```python
import jax
import jax.numpy as jnp
from jax import lax
from jax.sharding import PartitionSpec as P

PANEL = 512
NPANEL = 2
STAIR_BLOCK = 128


def spread(value, axis, source):
    kept = jnp.where(lax.axis_index(axis) == source, value, 0).astype(value.dtype)
    return lax.psum(kept, axis)


def pack_rows(values, targets, groups):
    rows_dev = values.shape[0]
    base_rows = 3 * rows_dev // (4 * groups)
    capacity = rows_dev - base_rows * (groups - 1)
    target_dev = targets // rows_dev
    target_row = targets % rows_dev
    onehot = (target_dev[:, None] == jnp.arange(groups, dtype=jnp.int32)[None, :]).astype(jnp.int32)
    rank_within = jnp.sum((jnp.cumsum(onehot, axis=0) - onehot) * onehot, axis=1)
    buffer_index = target_dev * capacity + rank_within
    source_row = (
        jnp.full((groups * capacity,), rows_dev, jnp.int32)
        .at[buffer_index]
        .set(jnp.arange(rows_dev, dtype=jnp.int32))
    )
    sent_rows = jnp.take(values, source_row, axis=0, mode="fill", fill_value=0.0)
    sent_slots = (
        jnp.full((groups * capacity,), rows_dev, jnp.int32).at[buffer_index].set(target_row)
    )
    return (
        sent_rows.reshape(groups, capacity, values.shape[1]),
        sent_slots.reshape(groups, capacity),
    )


def place_rows(recv_rows, recv_slots, rows_dev):
    flat_rows = recv_rows.reshape(-1, recv_rows.shape[-1])
    flat_slots = recv_slots.reshape(-1)
    where_from = (
        jnp.zeros((rows_dev,), jnp.int32)
        .at[flat_slots]
        .set(jnp.arange(flat_slots.shape[0], dtype=jnp.int32), mode="drop")
    )
    return jnp.take(flat_rows, where_from, axis=0)


def matmul(left, right):
    return jnp.dot(left, right, precision=lax.Precision.HIGHEST, preferred_element_type=jnp.float32)


def high(left, right, contract):
    return lax.dot_general(
        left,
        right,
        (contract, ((), ())),
        precision=lax.Precision.HIGH,
        preferred_element_type=jnp.float32,
    )


def cholesky_inverse(gram):
    lower = jnp.linalg.cholesky(gram)
    eye = jnp.eye(gram.shape[0], dtype=gram.dtype)
    return jax.scipy.linalg.solve_triangular(lower, eye, lower=True)


def gram_inverse_factor(g00, g10, g11):
    i00 = cholesky_inverse(g00)
    l10 = matmul(g10, i00.T)
    i11 = cholesky_inverse(g11 - matmul(l10, l10.T))
    i10 = -matmul(i11, matmul(l10, i00))
    return jnp.concatenate(
        [jnp.concatenate([i00, jnp.zeros_like(i00)], 1), jnp.concatenate([i10, i11], 1)], 0
    )


def shards(child_rows, row_map, stair):
    groups = lax.axis_size("gr")
    rows_dev, cols_dev = child_rows.shape
    wide = NPANEL * PANEL
    half = PANEL // 2
    columns = lax.axis_index("gc") * cols_dev + jnp.arange(cols_dev, dtype=jnp.int32)
    limits = jnp.take(stair, row_map // STAIR_BLOCK)
    masked = jnp.where(columns[None, :] >= limits[:, None], child_rows, jnp.zeros_like(child_rows))
    own = masked[:, :wide]
    left = matmul(own.T, own[:, :PANEL])
    low = matmul(own[:, PANEL:].T, own[:, PANEL:])
    low = jnp.concatenate([low[:, :half], low[:, half:]], axis=0)
    gram = jnp.concatenate([left, low], axis=1)
    gram = jnp.where(lax.axis_index("gc") == 0, gram, jnp.zeros_like(gram))
    gram, masked, own = lax.optimization_barrier((gram, masked, own))
    gram = lax.psum(gram, ("gr", "gc"))
    sent_rows, sent_slots = pack_rows(masked, row_map, groups)
    recv_rows, recv_slots = (
        lax.all_to_all(sent_rows, "gr", split_axis=0, concat_axis=0, tiled=True),
        lax.all_to_all(sent_slots, "gr", split_axis=0, concat_axis=0, tiled=True),
    )
    own, gram = lax.optimization_barrier((own, gram))
    panel = spread(own, "gc", 0)
    local = high(panel, masked, ((0,), (0,)))
    products = lax.psum(local, "gr")
    low = jnp.concatenate([gram[:PANEL, PANEL:], gram[PANEL:, PANEL:]], axis=1)
    inverse = gram_inverse_factor(gram[:PANEL, :PANEL], gram[PANEL:, :PANEL], low)
    front = place_rows(recv_rows, recv_slots, rows_dev)
    front_own, _ = lax.optimization_barrier((front[:, :wide], local))
    front_panel = spread(front_own, "gc", 0)
    basis = high(front_panel, inverse, ((1,), (1,)))
    stacked = high(inverse, products, ((1,), (0,)))
    projected = front - high(basis, stacked, ((1,), (0,)))
    share_rows = wide // groups
    factor = lax.dynamic_slice_in_dim(stacked, lax.axis_index("gr") * share_rows, share_rows, 0)
    return (factor, projected)


def solution(mesh):
    placed = (P("gr", "gc"), P("gr"), P())
    return jax.shard_map(
        shards,
        mesh=mesh,
        in_specs=placed,
        out_specs=(P("gr", "gc"), P("gr", "gc")),
        check_vma=False,
    )
```

profile of v0, /device:TPU:1, one launch (start us, length us, event | category | flops | bytes accessed | tf_op | source)
XLA Modules:
  0.0 959.6 jit_solution(5072844450119974676)
XLA Ops:
  9.4 2.5 scatter_custom_fusion
  12.6 7.6 all-to-all-start
  28.0 40.5 %select_select_fusion.2 = s32[512]{0:T(512)S(1)} fusion(s32[512]{0:T(512)} %param.7, s32[]{:T(128)} %bitcast, s32[]{:T(128)} %bitcast.1, s32[]{:T(128)} %bitcast.2, s32[]{:T(128)} %bitcast.3, s32[]{:T(128)} %bitcast.4, s32[]{:T(128)} %bitcast.5, s32[]{:T(128)} %bitcast.6, s32[]{:T(128)} %bitcast.7, s32[]{:T(128)} %bitcast.8, s32[]{:T(128)} %bitcast.9, ...), kind=kLoop, calls=%fused_computation.171 | loop fusion | flops 75776 | bytes 4352 | tf_op jit(solution)/shard_map/jit(_take)/select_n | solution.py:87
  70.7 2.9 fusion.2
  73.6 4.9 fusion.4
  78.5 2.5 scatter_custom_fusion.2
  84.9 10.1 %gather_fusion = f32[2432,1536]{1,0:T(8,128)} fusion(f32[512,1536]{1,0:T(8,128)S(1)} %compare_select_fusion, s32[3072]{0:T(1024)S(1)} %pad_clamp_fusion), kind=kCustom, calls=%fused_computation | custom fusion | bytes 29894144 | tf_op jit(solution)/shard_map/jit(_take)/gather | solution.py:30
  95.0 11.6 %broadcast_select_fusion = f32[16,152,1536]{2,1,0:T(8,128)} fusion(f32[16,152,1536]{2,1,0:T(8,128)} %bitcast.192, pred[16,152]{1,0:T(8,128)(4,1)S(1)} %broadcast_in_dim.63), kind=kLoop, calls=%fused_computation.9 | loop fusion | flops 3735552 | bytes 29886848 | tf_op jit(solution)/shard_map/jit(_take)/select_n | solution.py:30
  106.6 6.7 all-to-all-start.1
  114.4 12.8 %scatter_custom_fusion.1 = s32[512]{0:T(512)S(1)} fusion(s32[2432]{0:T(1024)S(1)} %fusion.76, s32[2432]{0:T(1024)S(1)} %iota.96, s32[]{:T(128)} %copy.55), kind=kCustom, calls=%fused_computation.190 | custom fusion | bytes 2052 | tf_op jit(solution)/shard_map/scatter | solution.py:46
  127.3 373.6 %all-reduce.7.cloned.1.call-done = f32[1024,768]{0,1:T(8,128)} async-done(((f32[1024,768]{0,1:T(8,128)}), f32[1024,768]{0,1:T(8,128)}) %all-reduce.7.cloned.1.call-update) | async-done | bytes 3145744 | tf_op jit(solution)/shard_map/psum | solution.py:96
  503.9 11.7 %cholesky.286 = f32[128,128]{1,0:T(8,128)S(1)} custom-call(f32[128,128]{1,0:T(8,128)S(1)} %cholesky.426), custom_call_target="Cholesky" | custom-call | tf_op jit(solution)/shard_map/jit(cholesky)/cholesky | solution.py:66
  516.8 9.8 %custom-call.27 = f32[1,128,128]{1,2,0:T(8,128)S(1)} custom-call(f32[1,128,128]{2,1,0:T(8,128)S(1)} %get-tuple-element.75), custom_call_target="InvertDiagBlocksLowerTriangular" | custom-call | tf_op jit(solution)/shard_map/jit(cholesky)/cholesky | solution.py:66
  529.0 11.7 %cholesky.305 = f32[128,128]{1,0:T(8,128)S(1)} custom-call(f32[128,128]{1,0:T(8,128)S(1)} %cholesky.430), custom_call_target="Cholesky" | custom-call | tf_op jit(solution)/shard_map/jit(cholesky)/cholesky | solution.py:66
  541.4 10.0 %custom-call.28 = f32[1,128,128]{1,2,0:T(8,128)S(1)} custom-call(f32[1,128,128]{2,1,0:T(8,128)S(1)} %get-tuple-element.72), custom_call_target="InvertDiagBlocksLowerTriangular" | custom-call | tf_op jit(solution)/shard_map/jit(cholesky)/cholesky | solution.py:66
  553.7 11.7 %cholesky.326 = f32[128,128]{1,0:T(8,128)S(1)} custom-call(f32[128,128]{1,0:T(8,128)S(1)} %cholesky.435), custom_call_target="Cholesky" | custom-call | tf_op jit(solution)/shard_map/jit(cholesky)/cholesky | solution.py:66
  566.1 9.8 %custom-call.29 = f32[1,128,128]{1,2,0:T(8,128)S(1)} custom-call(f32[1,128,128]{2,1,0:T(8,128)S(1)} %get-tuple-element.69), custom_call_target="InvertDiagBlocksLowerTriangular" | custom-call | tf_op jit(solution)/shard_map/jit(cholesky)/cholesky | solution.py:66
  578.2 11.7 %cholesky.343 = f32[128,128]{1,0:T(8,128)S(1)} custom-call(f32[128,128]{1,0:T(8,128)S(1)} %convolution_subtract_fusion.13), custom_call_target="Cholesky" | custom-call | tf_op jit(solution)/shard_map/jit(cholesky)/cholesky | solution.py:66
  595.3 2.3 select_select_fusion.1
  597.7 11.8 %while.4 = (s32[]{:T(128)}, f32[512,512]{1,0:T(8,128)}, s32[4,2]{0,1:T(2,128)S(1)}, f32[4,128,128]{2,1,0:T(8,128)S(1)}, s32[]{:T(128)}) while((s32[]{:T(128)}, f32[512,512]{1,0:T(8,128)}, s32[4,2]{0,1:T(2,128)S(1)}, f32[4,128,128]{2,1,0:T(8,128)S(1)}, s32[]{:T(128)}) %tuple.124), condition=%wide.while_cond, body=%wide.while_body.sunk | while | flops 2 | bytes 131181 | solution.py:68
  601.3 2.3 bitcast_dynamic-update-slice_fusion.4
  604.3 2.3 bitcast_dynamic-update-slice_fusion.4
  609.5 39.9 %custom-call.30 = f32[4,128,128]{1,2,0:T(8,128)} custom-call(f32[4,128,128]{2,1,0:T(8,128)S(1)} %get-tuple-element.30), custom_call_target="InvertDiagBlocksLowerTriangular" | custom-call | tf_op jit(solution)/shard_map/jit(_solve_triangular)/triangular_solve | solution.py:68
  658.1 3.6 fusion.15
  662.7 2.9 convolution_subtract_fusion.1
  665.5 2.6 copy.15
  668.2 45.4 %all-reduce.9.cloned.1.call-done = f32[512,1024]{1,0:T(8,128)} async-done(((f32[512,1024]{1,0:T(8,128)}), f32[512,1024]{1,0:T(8,128)}) %all-reduce.9.cloned.1.call-update) | async-done | bytes 2097168 | tf_op jit(solution)/shard_map/psum | solution.py:13
  713.5 9.2 fusion.105
  722.7 9.8 %gather_fusion.1 = f32[512,1536]{1,0:T(8,128)} fusion(f32[2432,1536]{1,0:T(8,128)} %bitcast.89, s32[1024]{0:T(1024)S(1)} %pad_clamp_fusion.1), kind=kCustom, calls=%fused_computation.1 | custom fusion | bytes 6293504 | tf_op jit(solution)/shard_map/jit(_take)/gather | solution.py:48
  739.4 11.7 %cholesky.358 = f32[128,128]{1,0:T(8,128)S(1)} custom-call(f32[128,128]{1,0:T(8,128)S(1)} %cholesky.439), custom_call_target="Cholesky" | custom-call | tf_op jit(solution)/shard_map/jit(cholesky)/cholesky | solution.py:66
  752.3 9.8 %custom-call.31 = f32[1,128,128]{1,2,0:T(8,128)S(1)} custom-call(f32[1,128,128]{2,1,0:T(8,128)S(1)} %get-tuple-element.65), custom_call_target="InvertDiagBlocksLowerTriangular" | custom-call | tf_op jit(solution)/shard_map/jit(cholesky)/cholesky | solution.py:66
  766.0 11.7 %cholesky.377 = f32[128,128]{1,0:T(8,128)S(1)} custom-call(f32[128,128]{1,0:T(8,128)S(1)} %cholesky.443), custom_call_target="Cholesky" | custom-call | tf_op jit(solution)/shard_map/jit(cholesky)/cholesky | solution.py:66
  778.3 10.0 %custom-call.32 = f32[1,128,128]{1,2,0:T(8,128)S(1)} custom-call(f32[1,128,128]{2,1,0:T(8,128)S(1)} %get-tuple-element.62), custom_call_target="InvertDiagBlocksLowerTriangular" | custom-call | tf_op jit(solution)/shard_map/jit(cholesky)/cholesky | solution.py:66
  792.2 13.2 %cholesky.398 = f32[128,128]{1,0:T(8,128)} custom-call(f32[128,128]{1,0:T(8,128)} %cholesky.448), custom_call_target="Cholesky" | custom-call | tf_op jit(solution)/shard_map/jit(cholesky)/cholesky | solution.py:66
  806.9 11.3 %custom-call.33 = f32[1,128,128]{1,2,0:T(8,128)} custom-call(f32[1,128,128]{2,1,0:T(8,128)} %get-tuple-element.59), custom_call_target="InvertDiagBlocksLowerTriangular" | custom-call | tf_op jit(solution)/shard_map/jit(cholesky)/cholesky | solution.py:66
  821.3 11.7 %cholesky.415 = f32[128,128]{1,0:T(8,128)S(1)} custom-call(f32[128,128]{1,0:T(8,128)S(1)} %convolution_subtract_fusion.12), custom_call_target="Cholesky" | custom-call | tf_op jit(solution)/shard_map/jit(cholesky)/cholesky | solution.py:66
  839.2 2.3 select_select_fusion
  842.3 13.9 %while.5 = (s32[]{:T(128)}, f32[512,512]{1,0:T(8,128)}, s32[4,2]{0,1:T(2,128)S(1)}, f32[4,128,128]{2,1,0:T(8,128)}, s32[]{:T(128)}) while((s32[]{:T(128)}, f32[512,512]{1,0:T(8,128)}, s32[4,2]{0,1:T(2,128)S(1)}, f32[4,128,128]{2,1,0:T(8,128)}, s32[]{:T(128)}) %tuple.138), condition=%wide.while_cond.clone, body=%wide.while_body.clone.sunk | while | flops 2 | bytes 132705 | solution.py:68
  843.3 2.8 bitcast_dynamic-update-slice_fusion.5
  846.7 2.8 bitcast_dynamic-update-slice_fusion.5
  850.1 2.8 bitcast_dynamic-update-slice_fusion.5
  853.5 2.7 bitcast_dynamic-update-slice_fusion.5
  856.2 40.7 %custom-call.34 = f32[4,128,128]{1,2,0:T(8,128)} custom-call(f32[4,128,128]{2,1,0:T(8,128)} %get-tuple-element.31), custom_call_target="InvertDiagBlocksLowerTriangular" | custom-call | tf_op jit(solution)/shard_map/jit(_solve_triangular)/triangular_solve | solution.py:68
  908.7 2.8 convolution_negate_fusion
  911.6 8.0 fusion
  919.6 10.1 %all-reduce.11.cloned.1.call-done = f32[1024,1536]{1,0:T(8,128)} async-done(((f32[1024,1536]{1,0:T(8,128)}), f32[1024,1536]{1,0:T(8,128)}) %all-reduce.11.cloned.1.call-update) | async-done | bytes 6291472 | tf_op jit(solution)/shard_map/psum | solution.py:105
  929.7 15.2 %fusion.1 = f32[1024,1536]{1,0:T(8,128)S(1)} fusion(f32[1024,1536]{1,0:T(8,128)} %all-reduce.11.cloned.1.call-done, f32[512,512]{1,0:T(8,128)} %pad_maximum_fusion, f32[128,512]{1,0:T(8,128)} %copy-done.21, f32[128,512]{1,0:T(8,128)} %copy-done.19, f32[128,512]{1,0:T(8,128)} %copy-done.16, f32[128,512]{1,0:T(8,128)S(1)} %copy-done.10, ...), kind=kOutput, calls=%fused_computation.17 | convolution fusion | flops 9671016448 | bytes 15728640 | tf_op jit(solution)/shard_map/dot_general | solution.py:56
  944.9 7.2 convolution_subtract_fusion
  (176 shorter events, 90.1 us)
Async XLA Ops:
  12.6 94.0 %all-to-all-start = ((s32[16,1,152]{2,1,0:T(1,128)}), s32[16,1,152]{2,1,0:T(1,128)S(1)}, u32[]{:S(2)}, u32[]{:S(2)}) async-start(s32[16,1,152]{2,1,0:T(1,128)} %all_to_all.9), calls=%async_computation | async-start | bytes 32768 | tf_op jit(solution)/shard_map/all_to_all | solution.py:100
  70.7 14.2 %copy-start = (f32[512,1536]{1,0:T(8,128)}, f32[512,1536]{1,0:T(8,128)S(1)}, u32[]{:S(2)}) copy-start(f32[512,1536]{1,0:T(8,128)S(1)} %compare_select_fusion) | copy-start | bytes 9437188
  80.9 1.9 copy-start.8
  106.6 616.1 %all-to-all-start.1 = ((f32[16,152,1536]{2,1,0:T(8,128)}), f32[16,152,1536]{2,1,0:T(8,128)}, u32[]{:S(2)}, u32[]{:S(2)}) async-start(f32[16,152,1536]{2,1,0:T(8,128)} %broadcast_select_fusion), calls=%async_computation.1 | async-start | bytes 29884416 | tf_op jit(solution)/shard_map/all_to_all | solution.py:99
  113.3 387.5 %all-reduce.7.cloned.1.call-start = ((), (), s32[]{:S(2)}) async-start(), calls=%async_computation.2 | async-start | bytes 6291456 | tf_op jit(solution)/shard_map/psum | solution.py:96
  114.0 599.5 %all-reduce.9.cloned.1.call-start = ((), (), s32[]{:S(2)}) async-start(), calls=%async_computation.3 | async-start | bytes 4194304 | tf_op jit(solution)/shard_map/psum | solution.py:13
  114.2 541.7 %copy-start.4 = (f32[512,512]{1,0:T(8,128)}, f32[512,512]{1,0:T(8,128)S(1)}, u32[]{:S(2)}) copy-start(f32[512,512]{1,0:T(8,128)S(1)} %fusion.17) | copy-start | bytes 3145732
  503.9 22.7 %copy-start.18 = (f32[512,512]{1,0:T(8,128)}, f32[512,512]{1,0:T(8,128)S(1)}, u32[]{:S(2)}) copy-start(f32[512,512]{1,0:T(8,128)S(1)} %fusion.14) | copy-start | bytes 3145732
  527.6 121.8 %slice-start = ((f32[512,1536]{1,0:T(8,128)}), f32[512,1024]{1,0:T(8,128)S(1)}, s32[]{:S(2)}) async-start(f32[512,1536]{1,0:T(8,128)} %copy-done), calls=%async_computation.6 | async-start | bytes 4194304 | tf_op jit(solution)/shard_map/slice | solution.py:89
  650.9 2.7 copy-start.23
  650.9 260.7 %all-reduce.13.cloned.1.call-start = ((), (), s32[]{:S(2)}) async-start(), calls=%async_computation.5 | async-start | bytes 4194304 | tf_op jit(solution)/shard_map/psum | solution.py:13
  650.9 7.1 copy-start.13
  654.0 7.6 copy-start.6
  655.9 5.8 copy-start.11
  658.0 3.7 copy-start.14
  661.7 1.0 copy-start.2
  662.7 50.9 %copy-start.1 = (f32[512,1536]{1,0:T(8,128)S(1)}, f32[512,1536]{1,0:T(8,128)}, u32[]{:S(2)}) copy-start(f32[512,1536]{1,0:T(8,128)} %copy-done) | copy-start | bytes 9437188
  736.4 193.3 %all-reduce.11.cloned.1.call-start = ((), (), s32[]{:S(2)}) async-start(), calls=%async_computation.4 | async-start | bytes 12582912 | tf_op jit(solution)/shard_map/psum | solution.py:105
  738.4 1.0 copy-start.17
  765.3 0.7 copy-start.22
  897.0 5.4 copy-start.24
  897.0 5.8 copy-start.5
  899.2 7.6 copy-start.3
  899.2 7.6 copy-start.7
  899.2 7.6 copy-start.12
  899.2 7.6 copy-start.15
  900.8 7.9 copy-start.9
  902.8 5.9 copy-start.16
  904.7 4.0 copy-start.19
  906.8 1.9 copy-start.21
  911.6 18.1 %copy-start.10 = (f32[128,512]{1,0:T(8,128)S(1)}, f32[128,512]{1,0:T(8,128)}, u32[]{:S(2)}) copy-start(f32[128,512]{1,0:T(8,128)} %copy-done.9) | copy-start | bytes 786436
  929.7 15.2 %copy-start.20 = (f32[512,1024]{1,0:T(8,128)S(1)}, f32[512,1024]{1,0:T(8,128)}, u32[]{:S(2)}) copy-start(f32[512,1024]{1,0:T(8,128)} %fusion) | copy-start | bytes 6291460
Sparse Core Ops, SparseCore 0:
  118.9 381.9 all-reduce.6
  651.0 62.4 all-reduce.8
  736.5 65.7 all-reduce.12
  806.0 123.6 all-reduce.10
where the time goes:
time: 972 us; the launch traced here: 960 us
  waiting for transfers between devices  430 us (44%)
  other arithmetic  320 us (33%)
  matrix products  89.4 us (9%)
  local copies, waits for them, and re-layouts  85.2 us (9%)
  between operations  20 us (2%)
  starting transfers between devices  14.6 us (2%)
    psum x1, waiting for transfers between devices, shards(): gram = lax.psum(gram, ('gr', 'gc'))  374 us
    another operation x29, other arithmetic, cholesky_inverse(): lower = jnp.linalg.cholesky(gram)  166 us
    another operation x6, other arithmetic, cholesky_inverse(): return jax.scipy.linalg.solve_triangular(lower, eye, lower=True)  87.6 us
    psum x2, waiting for transfers between devices, spread(): return lax.psum(kept, axis)  45.4 us
    select_n x1, other arithmetic, shards(): limits = jnp.take(stair, row_map // STAIR_BLOCK)  40.5 us
    dot_general x4, matrix products, high(): lax.dot_general(left, right, (contract, ((), ())), precision=lax.Precisio...  39.7 us
    another operation x27, local copies, waits for them, and re-layouts, cholesky_inverse(): return jax.scipy.linalg.solve_triangular(lower, eye, lower=True)  26 us
  transfers between devices with their start and end apart: 6, of which 3 were waited for; matrix products, arithmetic and copies ran while one was open for 47% of the time, Pallas kernels for 0%

commit v1 on v0

--- a/solution.py
+++ b/solution.py
@@ -93,7 +93,8 @@
     gram = jnp.concatenate([left, low], axis=1)
     gram = jnp.where(lax.axis_index("gc") == 0, gram, jnp.zeros_like(gram))
     gram, masked, own = lax.optimization_barrier((gram, masked, own))
-    gram = lax.psum(gram, ("gr", "gc"))
+    inner = lax.psum(gram, "gc")
+    gram = lax.psum(inner, "gr")
     sent_rows, sent_slots = pack_rows(masked, row_map, groups)
     recv_rows, recv_slots = (
         lax.all_to_all(sent_rows, "gr", split_axis=0, concat_axis=0, tiled=True),

time: 972 us -> 907 us (0.933)
  waiting for transfers between devices: 430 us -> 365 us
    psum x1 -> x2, waiting for transfers between devices: 374 us -> 308 us  [the longest x1 233 us: shards(): gram = lax.psum(inner, 'gr')]
  transfers between devices with their start and end apart: 6 -> 7, of which waited for: 3 -> 4; matrix products, arithmetic and copies ran while one was open for 47% -> 50% of each run, Pallas kernels for 0% -> 0%
where the time goes in v1:
time: 907 us; the launch traced here: 895 us
  waiting for transfers between devices  365 us (40%)
  other arithmetic  320 us (35%)
  matrix products  89.4 us (10%)
  local copies, waits for them, and re-layouts  85.2 us (9%)
  between operations  20 us (2%)
  starting transfers between devices  14.7 us (2%)
    psum x1, waiting for transfers between devices, shards(): gram = lax.psum(inner, 'gr')  233 us
    another operation x29, other arithmetic, cholesky_inverse(): lower = jnp.linalg.cholesky(gram)  166 us
    another operation x6, other arithmetic, cholesky_inverse(): return jax.scipy.linalg.solve_triangular(lower, eye, lower=True)  87.6 us
    psum x1, waiting for transfers between devices, shards(): inner = lax.psum(gram, 'gc')  74.6 us
    psum x2, waiting for transfers between devices, spread(): return lax.psum(kept, axis)  46.4 us
    select_n x1, other arithmetic, shards(): limits = jnp.take(stair, row_map // STAIR_BLOCK)  40.5 us
    dot_general x4, matrix products, high(): lax.dot_general(left, right, (contract, ((), ())), precision=lax.Precisio...  39.7 us
    another operation x27, local copies, waits for them, and re-layouts, cholesky_inverse(): return jax.scipy.linalg.solve_triangular(lower, eye, lower=True)  26 us
  transfers between devices with their start and end apart: 7, of which 4 were waited for; matrix products, arithmetic and copies ran while one was open for 50% of the time, Pallas kernels for 0%

profile of v1, /device:TPU:1, one launch (start us, length us, event | category | flops | bytes accessed | tf_op | source)
XLA Modules:
  0.0 895.0 jit_solution(11313348866431716438)
XLA Ops:
  9.4 2.5 scatter_custom_fusion
  12.6 7.6 all-to-all-start
  28.0 40.5 %select_select_fusion.2 = s32[512]{0:T(512)S(1)} fusion(s32[512]{0:T(512)} %param.7, s32[]{:T(128)} %bitcast, s32[]{:T(128)} %bitcast.1, s32[]{:T(128)} %bitcast.2, s32[]{:T(128)} %bitcast.3, s32[]{:T(128)} %bitcast.4, s32[]{:T(128)} %bitcast.5, s32[]{:T(128)} %bitcast.6, s32[]{:T(128)} %bitcast.7, s32[]{:T(128)} %bitcast.8, s32[]{:T(128)} %bitcast.9, ...), kind=kLoop, calls=%fused_computation.171 | loop fusion | flops 75776 | bytes 4352 | tf_op jit(solution)/shard_map/jit(_take)/select_n | solution.py:87
  70.7 2.9 fusion.2
  73.6 4.9 fusion.4
  78.5 2.5 scatter_custom_fusion.2
  84.9 10.1 %gather_fusion = f32[2432,1536]{1,0:T(8,128)} fusion(f32[512,1536]{1,0:T(8,128)S(1)} %compare_select_fusion, s32[3072]{0:T(1024)S(1)} %pad_clamp_fusion), kind=kCustom, calls=%fused_computation | custom fusion | bytes 29894144 | tf_op jit(solution)/shard_map/jit(_take)/gather | solution.py:30
  95.0 11.6 %broadcast_select_fusion = f32[16,152,1536]{2,1,0:T(8,128)} fusion(f32[16,152,1536]{2,1,0:T(8,128)} %bitcast.192, pred[16,152]{1,0:T(8,128)(4,1)S(1)} %broadcast_in_dim.63), kind=kLoop, calls=%fused_computation.9 | loop fusion | flops 3735552 | bytes 29886848 | tf_op jit(solution)/shard_map/jit(_take)/select_n | solution.py:30
  106.6 6.7 all-to-all-start.1
  114.1 74.6 %all-reduce.8.cloned.1.call-done = f32[1024,768]{0,1:T(8,128)} async-done(((f32[1024,768]{0,1:T(8,128)}), f32[1024,768]{0,1:T(8,128)}) %all-reduce.8.cloned.1.call-update) | async-done | bytes 3145744 | tf_op jit(solution)/shard_map/psum | solution.py:96
  189.1 12.8 %scatter_custom_fusion.1 = s32[512]{0:T(512)S(1)} fusion(s32[2432]{0:T(1024)S(1)} %fusion.76, s32[2432]{0:T(1024)S(1)} %iota.96, s32[]{:T(128)} %copy.56), kind=kCustom, calls=%fused_computation.190 | custom fusion | bytes 2052 | tf_op jit(solution)/shard_map/scatter | solution.py:46
  202.0 233.3 %all-reduce.10.cloned.1.call-done = f32[1024,768]{0,1:T(8,128)} async-done(((f32[1024,768]{0,1:T(8,128)}), f32[1024,768]{0,1:T(8,128)}) %all-reduce.10.cloned.1.call-update) | async-done | bytes 3145744 | tf_op jit(solution)/shard_map/psum | solution.py:97
  438.4 11.7 %cholesky.286 = f32[128,128]{1,0:T(8,128)S(1)} custom-call(f32[128,128]{1,0:T(8,128)S(1)} %cholesky.426), custom_call_target="Cholesky" | custom-call | tf_op jit(solution)/shard_map/jit(cholesky)/cholesky | solution.py:66
  451.3 9.8 %custom-call.27 = f32[1,128,128]{1,2,0:T(8,128)S(1)} custom-call(f32[1,128,128]{2,1,0:T(8,128)S(1)} %get-tuple-element.75), custom_call_target="InvertDiagBlocksLowerTriangular" | custom-call | tf_op jit(solution)/shard_map/jit(cholesky)/cholesky | solution.py:66
  463.5 11.7 %cholesky.305 = f32[128,128]{1,0:T(8,128)S(1)} custom-call(f32[128,128]{1,0:T(8,128)S(1)} %cholesky.430), custom_call_target="Cholesky" | custom-call | tf_op jit(solution)/shard_map/jit(cholesky)/cholesky | solution.py:66
  475.9 10.0 %custom-call.28 = f32[1,128,128]{1,2,0:T(8,128)S(1)} custom-call(f32[1,128,128]{2,1,0:T(8,128)S(1)} %get-tuple-element.72), custom_call_target="InvertDiagBlocksLowerTriangular" | custom-call | tf_op jit(solution)/shard_map/jit(cholesky)/cholesky | solution.py:66
  488.2 11.7 %cholesky.326 = f32[128,128]{1,0:T(8,128)S(1)} custom-call(f32[128,128]{1,0:T(8,128)S(1)} %cholesky.435), custom_call_target="Cholesky" | custom-call | tf_op jit(solution)/shard_map/jit(cholesky)/cholesky | solution.py:66
  500.6 9.8 %custom-call.29 = f32[1,128,128]{1,2,0:T(8,128)S(1)} custom-call(f32[1,128,128]{2,1,0:T(8,128)S(1)} %get-tuple-element.69), custom_call_target="InvertDiagBlocksLowerTriangular" | custom-call | tf_op jit(solution)/shard_map/jit(cholesky)/cholesky | solution.py:66
  512.6 11.7 %cholesky.343 = f32[128,128]{1,0:T(8,128)S(1)} custom-call(f32[128,128]{1,0:T(8,128)S(1)} %convolution_subtract_fusion.13), custom_call_target="Cholesky" | custom-call | tf_op jit(solution)/shard_map/jit(cholesky)/cholesky | solution.py:66
  529.8 2.3 select_select_fusion.1
  532.1 11.8 %while.4 = (s32[]{:T(128)}, f32[512,512]{1,0:T(8,128)}, s32[4,2]{0,1:T(2,128)S(1)}, f32[4,128,128]{2,1,0:T(8,128)S(1)}, s32[]{:T(128)}) while((s32[]{:T(128)}, f32[512,512]{1,0:T(8,128)}, s32[4,2]{0,1:T(2,128)S(1)}, f32[4,128,128]{2,1,0:T(8,128)S(1)}, s32[]{:T(128)}) %tuple.124), condition=%wide.while_cond, body=%wide.while_body.sunk | while | flops 2 | bytes 131181 | solution.py:68
  532.8 2.3 bitcast_dynamic-update-slice_fusion.4
  543.9 39.9 %custom-call.30 = f32[4,128,128]{1,2,0:T(8,128)} custom-call(f32[4,128,128]{2,1,0:T(8,128)S(1)} %get-tuple-element.30), custom_call_target="InvertDiagBlocksLowerTriangular" | custom-call | tf_op jit(solution)/shard_map/jit(_solve_triangular)/triangular_solve | solution.py:68
  592.6 3.6 fusion.15
  597.1 2.9 convolution_subtract_fusion.1
  600.0 2.6 copy.15
  602.6 46.4 %all-reduce.12.cloned.1.call-done = f32[512,1024]{1,0:T(8,128)} async-done(((f32[512,1024]{1,0:T(8,128)}), f32[512,1024]{1,0:T(8,128)}) %all-reduce.12.cloned.1.call-update) | async-done | bytes 2097168 | tf_op jit(solution)/shard_map/psum | solution.py:13
  649.0 9.2 %fusion.105 = f32[1024,1536]{1,0:T(8,128)} fusion(f32[512,1024]{1,0:T(8,128)} %all-reduce.12.cloned.1.call-done, f32[512,1536]{1,0:T(8,128)S(1)} %copy-done.1), kind=kOutput, calls=%fused_computation.216 | convolution fusion | flops 4831838208 | bytes 11534336 | tf_op jit(solution)/shard_map/dot_general | solution.py:56
  658.3 9.8 %gather_fusion.1 = f32[512,1536]{1,0:T(8,128)} fusion(f32[2432,1536]{1,0:T(8,128)} %bitcast.89, s32[1024]{0:T(1024)S(1)} %pad_clamp_fusion.1), kind=kCustom, calls=%fused_computation.1 | custom fusion | bytes 6293504 | tf_op jit(solution)/shard_map/jit(_take)/gather | solution.py:48
  674.9 11.7 %cholesky.358 = f32[128,128]{1,0:T(8,128)S(1)} custom-call(f32[128,128]{1,0:T(8,128)S(1)} %cholesky.439), custom_call_target="Cholesky" | custom-call | tf_op jit(solution)/shard_map/jit(cholesky)/cholesky | solution.py:66
  687.8 9.8 %custom-call.31 = f32[1,128,128]{1,2,0:T(8,128)S(1)} custom-call(f32[1,128,128]{2,1,0:T(8,128)S(1)} %get-tuple-element.65), custom_call_target="InvertDiagBlocksLowerTriangular" | custom-call | tf_op jit(solution)/shard_map/jit(cholesky)/cholesky | solution.py:66
  701.5 11.7 %cholesky.377 = f32[128,128]{1,0:T(8,128)S(1)} custom-call(f32[128,128]{1,0:T(8,128)S(1)} %cholesky.443), custom_call_target="Cholesky" | custom-call | tf_op jit(solution)/shard_map/jit(cholesky)/cholesky | solution.py:66
  713.8 10.0 %custom-call.32 = f32[1,128,128]{1,2,0:T(8,128)S(1)} custom-call(f32[1,128,128]{2,1,0:T(8,128)S(1)} %get-tuple-element.62), custom_call_target="InvertDiagBlocksLowerTriangular" | custom-call | tf_op jit(solution)/shard_map/jit(cholesky)/cholesky | solution.py:66
  727.8 13.2 %cholesky.398 = f32[128,128]{1,0:T(8,128)} custom-call(f32[128,128]{1,0:T(8,128)} %cholesky.448), custom_call_target="Cholesky" | custom-call | tf_op jit(solution)/shard_map/jit(cholesky)/cholesky | solution.py:66
  742.4 11.3 %custom-call.33 = f32[1,128,128]{1,2,0:T(8,128)} custom-call(f32[1,128,128]{2,1,0:T(8,128)} %get-tuple-element.59), custom_call_target="InvertDiagBlocksLowerTriangular" | custom-call | tf_op jit(solution)/shard_map/jit(cholesky)/cholesky | solution.py:66
  756.8 11.7 %cholesky.415 = f32[128,128]{1,0:T(8,128)S(1)} custom-call(f32[128,128]{1,0:T(8,128)S(1)} %convolution_subtract_fusion.12), custom_call_target="Cholesky" | custom-call | tf_op jit(solution)/shard_map/jit(cholesky)/cholesky | solution.py:66
  774.7 2.3 select_select_fusion
  777.8 13.9 %while.5 = (s32[]{:T(128)}, f32[512,512]{1,0:T(8,128)}, s32[4,2]{0,1:T(2,128)S(1)}, f32[4,128,128]{2,1,0:T(8,128)}, s32[]{:T(128)}) while((s32[]{:T(128)}, f32[512,512]{1,0:T(8,128)}, s32[4,2]{0,1:T(2,128)S(1)}, f32[4,128,128]{2,1,0:T(8,128)}, s32[]{:T(128)}) %tuple.140), condition=%wide.while_cond.clone, body=%wide.while_body.clone.sunk | while | flops 2 | bytes 132705 | solution.py:68
  778.8 2.8 bitcast_dynamic-update-slice_fusion.5
  782.2 2.8 bitcast_dynamic-update-slice_fusion.5
  785.6 2.8 bitcast_dynamic-update-slice_fusion.5
  789.0 2.7 bitcast_dynamic-update-slice_fusion.5
  791.7 40.7 %custom-call.34 = f32[4,128,128]{1,2,0:T(8,128)} custom-call(f32[4,128,128]{2,1,0:T(8,128)} %get-tuple-element.31), custom_call_target="InvertDiagBlocksLowerTriangular" | custom-call | tf_op jit(solution)/shard_map/jit(_solve_triangular)/triangular_solve | solution.py:68
  844.3 2.8 convolution_negate_fusion
  847.1 8.0 fusion
  855.1 10.0 %all-reduce.14.cloned.1.call-done = f32[1024,1536]{1,0:T(8,128)} async-done(((f32[1024,1536]{1,0:T(8,128)}), f32[1024,1536]{1,0:T(8,128)}) %all-reduce.14.cloned.1.call-update) | async-done | bytes 6291472 | tf_op jit(solution)/shard_map/psum | solution.py:106
  865.1 15.2 %fusion.1 = f32[1024,1536]{1,0:T(8,128)S(1)} fusion(f32[1024,1536]{1,0:T(8,128)} %all-reduce.14.cloned.1.call-done, f32[512,512]{1,0:T(8,128)} %pad_maximum_fusion, f32[128,512]{1,0:T(8,128)} %copy-done.21, f32[128,512]{1,0:T(8,128)} %copy-done.19, f32[128,512]{1,0:T(8,128)} %copy-done.16, f32[128,512]{1,0:T(8,128)S(1)} %copy-done.10, ...), kind=kOutput, calls=%fused_computation.17 | convolution fusion | flops 9671016448 | bytes 15728640 | tf_op jit(solution)/shard_map/dot_general | solution.py:56
  880.3 7.2 convolution_subtract_fusion
  (179 shorter events, 92.4 us)
Async XLA Ops:
  12.6 94.1 %all-to-all-start = ((s32[16,1,152]{2,1,0:T(1,128)}), s32[16,1,152]{2,1,0:T(1,128)S(1)}, u32[]{:S(2)}, u32[]{:S(2)}) async-start(s32[16,1,152]{2,1,0:T(1,128)} %all_to_all.9), calls=%async_computation | async-start | bytes 32768 | tf_op jit(solution)/shard_map/all_to_all | solution.py:101
  70.7 14.2 %copy-start = (f32[512,1536]{1,0:T(8,128)}, f32[512,1536]{1,0:T(8,128)S(1)}, u32[]{:S(2)}) copy-start(f32[512,1536]{1,0:T(8,128)S(1)} %compare_select_fusion) | copy-start | bytes 9437188
  80.9 1.9 copy-start.8
  106.6 551.6 %all-to-all-start.1 = ((f32[16,152,1536]{2,1,0:T(8,128)}), f32[16,152,1536]{2,1,0:T(8,128)}, u32[]{:S(2)}, u32[]{:S(2)}) async-start(f32[16,152,1536]{2,1,0:T(8,128)} %broadcast_select_fusion), calls=%async_computation.1 | async-start | bytes 29884416 | tf_op jit(solution)/shard_map/all_to_all | solution.py:100
  113.3 75.4 %all-reduce.8.cloned.1.call-start = ((), (), s32[]{:S(2)}) async-start(), calls=%async_computation.2 | async-start | bytes 6291456 | tf_op jit(solution)/shard_map/psum | solution.py:96
  114.1 321.2 %all-reduce.10.cloned.1.call-start = ((), (), s32[]{:S(2)}) async-start(), calls=%async_computation.3 | async-start | bytes 6291456 | tf_op jit(solution)/shard_map/psum | solution.py:97
  188.7 460.3 %all-reduce.12.cloned.1.call-start = ((), (), s32[]{:S(2)}) async-start(), calls=%async_computation.4 | async-start | bytes 4194304 | tf_op jit(solution)/shard_map/psum | solution.py:13
  188.9 401.4 %copy-start.4 = (f32[512,512]{1,0:T(8,128)}, f32[512,512]{1,0:T(8,128)S(1)}, u32[]{:S(2)}) copy-start(f32[512,512]{1,0:T(8,128)S(1)} %fusion.17) | copy-start | bytes 3145732
  438.4 22.7 %copy-start.18 = (f32[512,512]{1,0:T(8,128)}, f32[512,512]{1,0:T(8,128)S(1)}, u32[]{:S(2)}) copy-start(f32[512,512]{1,0:T(8,128)S(1)} %fusion.14) | copy-start | bytes 3145732
  462.1 121.8 %slice-start = ((f32[512,1536]{1,0:T(8,128)}), f32[512,1024]{1,0:T(8,128)S(1)}, s32[]{:S(2)}) async-start(f32[512,1536]{1,0:T(8,128)} %copy-done), calls=%async_computation.7 | async-start | bytes 4194304 | tf_op jit(solution)/shard_map/slice | solution.py:89
  585.3 2.7 copy-start.23
  585.4 261.7 %all-reduce.16.cloned.1.call-start = ((), (), s32[]{:S(2)}) async-start(), calls=%async_computation.6 | async-start | bytes 4194304 | tf_op jit(solution)/shard_map/psum | solution.py:13
  585.4 7.1 copy-start.13
  588.5 7.7 copy-start.6
  590.4 5.8 copy-start.11
  592.5 3.7 copy-start.14
  596.2 1.0 copy-start.2
  597.1 51.9 %copy-start.1 = (f32[512,1536]{1,0:T(8,128)S(1)}, f32[512,1536]{1,0:T(8,128)}, u32[]{:S(2)}) copy-start(f32[512,1536]{1,0:T(8,128)} %copy-done) | copy-start | bytes 9437188
  671.9 193.2 %all-reduce.14.cloned.1.call-start = ((), (), s32[]{:S(2)}) async-start(), calls=%async_computation.5 | async-start | bytes 12582912 | tf_op jit(solution)/shard_map/psum | solution.py:106
  673.9 1.0 copy-start.17
  700.8 0.7 copy-start.22
  832.5 5.4 copy-start.24
  832.5 5.8 copy-start.5
  834.8 7.6 copy-start.3
  834.8 7.6 copy-start.7
  834.8 7.6 copy-start.12
  834.8 7.6 copy-start.15
  836.4 7.9 copy-start.9
  838.3 5.9 copy-start.16
  840.2 4.0 copy-start.19
  842.3 1.9 copy-start.21
  847.1 18.0 %copy-start.10 = (f32[128,512]{1,0:T(8,128)S(1)}, f32[128,512]{1,0:T(8,128)}, u32[]{:S(2)}) copy-start(f32[128,512]{1,0:T(8,128)} %copy-done.9) | copy-start | bytes 786436
  865.1 15.2 %copy-start.20 = (f32[512,1024]{1,0:T(8,128)S(1)}, f32[512,1024]{1,0:T(8,128)}, u32[]{:S(2)}) copy-start(f32[512,1024]{1,0:T(8,128)} %fusion) | copy-start | bytes 6291460
Sparse Core Ops, SparseCore 0:
  116.5 72.1 all-reduce.7
  192.1 243.1 all-reduce.9
  585.5 63.5 all-reduce.11
  672.1 65.7 all-reduce.15
  741.1 123.9 all-reduce.13
